TPU v7x, 32 devices: a whole 2x2x4 slice. The times are simulated.
32 devices in a mesh: dp: 16 (over z, y, core), head: 2 (over x).
Axes of the slice: x: 2, y: 2, z: 4, core: 2. Of those that a mesh axis runs over, the one named last changes fastest.
Arguments:
- tokens: bfloat16 [2, 16384, 768], P(None, ('dp', 'head')), may hold values from -6 to 6
- segment_ids: int32 [2, 32, 512], P(None, 'dp'), may hold values from 0 to 15, never falling along the last dimension, each value on 1 to 256 neighbouring positions
- w_qkv: bfloat16 [3, 768, 768], P(None, 'dp', 'head'), may hold values from -0.21875 to 0.21875
- qv_bias: float32 [2, 768], replicated, may hold values from -3 to 3
- w_out: bfloat16 [768, 768], P(None, ('dp', 'head')), may hold values from -0.875 to 0.875
- out_bias: float32 [768], replicated, may hold values from -3 to 3
- w_in: bfloat16 [768, 3072], P(None, ('dp', 'head')), may hold values from -0.21875 to 0.21875
- in_bias: float32 [3072], replicated, may hold values from -3 to 3
- w_back: bfloat16 [3072, 768], P(None, ('dp', 'head')), may hold values from -0.109375 to 0.109375
- back_bias: float32 [768], replicated, may hold values from -3 to 3
- norm_gains: float32 [2, 768], replicated, may hold values from 0.25 to 1.75
- norm_shifts: float32 [2, 768], replicated, may hold values from -2 to 2
- out_cotangent: bfloat16 [2, 16384, 768], P(None, ('dp', 'head')), may hold values from -6 to 6
Outputs:
- out: bfloat16 [2, 16384, 768], P(None, ('dp', 'head'))
- x_grad: float32 [2, 16384, 768], P(None, ('dp', 'head'))
- w_qkv_grad: float32 [3, 768, 768], P(None, 'dp', 'head')
- qv_bias_grad: float32 [2, 768], replicated
- w_out_grad: float32 [768, 768], P(None, ('dp', 'head'))
- out_bias_grad: float32 [768], replicated
- w_in_grad: float32 [768, 3072], P(None, ('dp', 'head'))
- in_bias_grad: float32 [3072], replicated
- w_back_grad: float32 [3072, 768], P(None, ('dp', 'head'))
- back_bias_grad: float32 [768], replicated
- norm_gains_grad: float32 [2, 768], replicated
- norm_shifts_grad: float32 [2, 768], replicated
Inputs may be any that keep to these rules, and one draw needn't show every extreme that they name: `segment_ids`: within each packed row of 512 positions the ids never fall; a run of one id is at most 256 positions and one run in each row has that length.
All inputs are finite; a program needn't handle non-finite values.
Results may differ from a plain program's by a relative error of at most 0.014.
The roundings to bfloat16 on the way count: a program that leaves them out, or rounds other values in their place, can miss the bound.
Values may be sent and summed in bfloat16 or wider, within the bound.
A program may use at most 192 MiB of HBM per device.

v0:
```python
import jax
import jax.numpy as jnp
from jax import lax
from jax.sharding import PartitionSpec as P

HD = 64


NORM_EPS = 1e-05
MASKED = -1e30


def layer_norm(residual, norm_gain, offset):
    average = jnp.mean(residual, axis=-1, keepdims=True)
    centred = residual - average
    spread = jnp.mean(centred * centred, axis=-1, keepdims=True)
    return centred * lax.rsqrt(spread + NORM_EPS) * norm_gain + offset


def exact_gelu(inputs):
    return jax.nn.gelu(inputs, approximate=False)


def scores_of(queries, key_rows, segment):
    raw_scores = jnp.einsum("qhd,khd->hqk", queries, key_rows, preferred_element_type=jnp.float32)
    same_doc = segment[:, None] == segment[None, :]
    return jnp.where(same_doc[None], raw_scores * HD ** (-0.5), MASKED)


def attend_forward(block_items):
    queries, key_rows, values, segment = block_items
    scores = scores_of(queries, key_rows, segment)
    highest = jnp.max(scores, axis=-1, keepdims=True)
    exponent = jnp.exp(scores - highest)
    totals = jnp.sum(exponent, axis=-1, keepdims=True)
    probabilities = (exponent / totals).astype(jnp.bfloat16)
    context = jnp.einsum("hqk,khd->qhd", probabilities, values, preferred_element_type=jnp.float32)
    return (context.astype(jnp.bfloat16), highest[..., 0] + jnp.log(totals[..., 0]))


def attend_backward(block_items):
    queries, key_rows, values, segment, log_total, grad_context = block_items
    scores = scores_of(queries, key_rows, segment)
    probabilities = jnp.exp(scores - log_total[..., None])
    grad_probs = jnp.einsum(
        "qhd,khd->hqk", grad_context, values, preferred_element_type=jnp.float32
    )
    grad_values = jnp.einsum(
        "hqk,qhd->khd",
        probabilities.astype(jnp.bfloat16),
        grad_context,
        preferred_element_type=jnp.float32,
    )
    weighted = jnp.sum(probabilities * grad_probs, axis=-1, keepdims=True)
    grad_scores = (probabilities * (grad_probs - weighted)).astype(jnp.bfloat16)
    scale = HD ** (-0.5)
    grad_queries = (
        jnp.einsum("hqk,khd->qhd", grad_scores, key_rows, preferred_element_type=jnp.float32)
        * scale
    )
    grad_keys = (
        jnp.einsum("hqk,qhd->khd", grad_scores, queries, preferred_element_type=jnp.float32) * scale
    )
    return (
        grad_queries.astype(jnp.bfloat16),
        grad_keys.astype(jnp.bfloat16),
        grad_values.astype(jnp.bfloat16),
    )


def fetch_weights(w_qkv, w_out, w_in, w_back):
    head_full = lax.all_gather(w_qkv, "dp", axis=1, tiled=True)
    out_full, in_full, back_full = (
        lax.all_gather(w_out, ("dp", "head"), axis=1, tiled=True),
        lax.all_gather(w_in, ("dp", "head"), axis=1, tiled=True),
        lax.all_gather(w_back, ("dp", "head"), axis=1, tiled=True),
    )
    return (head_full, out_full, in_full, back_full)


def reduce_heads(head_term):
    return lax.psum_scatter(head_term, "dp", scatter_dimension=1, tiled=True)


def reduce_tokens(token_terms):
    return (
        lax.psum_scatter(token_terms[0], ("dp", "head"), scatter_dimension=1, tiled=True),
        lax.psum_scatter(token_terms[1], ("dp", "head"), scatter_dimension=1, tiled=True),
        lax.psum_scatter(token_terms[2], ("dp", "head"), scatter_dimension=1, tiled=True),
    )


def accumulate(total, term):
    if total is None:
        return term
    return jax.tree.map(jnp.add, total, term)


def on_device(
    tokens,
    segment_ids,
    w_qkv,
    qv_bias,
    w_out,
    out_bias,
    w_in,
    in_bias,
    w_back,
    back_bias,
    norm_gains,
    norm_shifts,
    out_cotangent,
):
    micro_count = tokens.shape[0]
    head_width = w_qkv.shape[2]
    head_count = head_width // HD
    seq_count = segment_ids.shape[1]
    seq_len = segment_ids.shape[2]
    head_start = lax.axis_index("head") * head_width
    bias_local = lax.dynamic_slice_in_dim(qv_bias, head_start, head_width, 1)
    head_shape = (seq_count, seq_len, head_count, HD)
    fetched = None
    head_total = None
    token_total = None
    small_total = None
    outputs = []
    input_grads = []
    for micro_idx in range(micro_count):
        fetched = fetch_weights(w_qkv, w_out, w_in, w_back)
        head_full, out_full, in_full, back_full = fetched
        x_local = tokens[micro_idx]
        x_group = lax.all_gather(x_local, "head", axis=0, tiled=True)
        projected = jnp.einsum(
            "td,cdf->ctf", x_group, head_full, preferred_element_type=jnp.float32
        )
        queries = (projected[0] + bias_local[0]).astype(jnp.bfloat16).reshape(head_shape)
        key_rows = projected[1].astype(jnp.bfloat16).reshape(head_shape)
        values = (projected[2] + bias_local[1]).astype(jnp.bfloat16).reshape(head_shape)
        segments = segment_ids[micro_idx]
        context, log_total = lax.map(attend_forward, (queries, key_rows, values, segments))
        context = context.reshape(seq_count * seq_len, head_width)
        ctx_tokens = lax.all_to_all(context, "head", split_axis=0, concat_axis=1, tiled=True)
        attended = jnp.dot(ctx_tokens, out_full, preferred_element_type=jnp.float32) + out_bias
        resid_one = x_local.astype(jnp.float32) + attended
        hidden, norm_first = jax.vjp(layer_norm, resid_one, norm_gains[0], norm_shifts[0])
        hidden_low = hidden.astype(jnp.bfloat16)
        pre_act = jnp.dot(hidden_low, in_full, preferred_element_type=jnp.float32) + in_bias
        activation, gelu_back = jax.vjp(exact_gelu, pre_act)
        activation_low = activation.astype(jnp.bfloat16)
        branch = jnp.dot(activation_low, back_full, preferred_element_type=jnp.float32) + back_bias
        result, norm_second = jax.vjp(layer_norm, hidden + branch, norm_gains[1], norm_shifts[1])
        outputs.append(result.astype(jnp.bfloat16))
        grad_two, gain_two, shift_two = norm_second(out_cotangent[micro_idx].astype(jnp.float32))
        grad_branch = grad_two.astype(jnp.bfloat16)
        back_term = jnp.einsum(
            "tf,td->fd", activation_low, grad_branch, preferred_element_type=jnp.float32
        )
        grad_act = jnp.einsum(
            "td,fd->tf", grad_branch, back_full, preferred_element_type=jnp.float32
        )
        grad_pre = gelu_back(grad_act)[0].astype(jnp.bfloat16)
        in_term = jnp.einsum("td,tf->df", hidden_low, grad_pre, preferred_element_type=jnp.float32)
        grad_hidden = grad_two + jnp.einsum(
            "tf,df->td", grad_pre, in_full, preferred_element_type=jnp.float32
        )
        grad_one, gain_one, shift_one = norm_first(grad_hidden)
        grad_attn = grad_one.astype(jnp.bfloat16)
        out_term = jnp.einsum(
            "tc,td->cd", ctx_tokens, grad_attn, preferred_element_type=jnp.float32
        )
        grad_ctx = jnp.einsum(
            "td,cd->tc", grad_attn, out_full, preferred_element_type=jnp.float32
        ).astype(jnp.bfloat16)
        grad_heads = lax.all_to_all(grad_ctx, "head", split_axis=1, concat_axis=0, tiled=True)
        grad_queries, grad_keys, grad_values = lax.map(
            attend_backward,
            (queries, key_rows, values, segments, log_total, grad_heads.reshape(head_shape)),
        )
        grad_proj = jnp.stack(
            [
                grad_queries.reshape(-1, head_width),
                grad_keys.reshape(-1, head_width),
                grad_values.reshape(-1, head_width),
            ]
        )
        head_term = jnp.einsum(
            "td,ctf->cdf", x_group, grad_proj, preferred_element_type=jnp.float32
        )
        grad_input = lax.psum_scatter(
            jnp.einsum(
                "ctf,cdf->td", grad_proj, head_full, preferred_element_type=jnp.float32
            ).astype(jnp.bfloat16),
            "head",
            scatter_dimension=0,
            tiled=True,
        ).astype(jnp.float32)
        input_grads.append(grad_one + grad_input)
        bias_heads = jnp.stack(
            [
                jnp.sum(grad_proj[0].astype(jnp.float32), axis=0),
                jnp.sum(grad_proj[2].astype(jnp.float32), axis=0),
            ]
        )
        bias_full = lax.dynamic_update_slice(
            jnp.zeros(qv_bias.shape, jnp.float32),
            bias_heads,
            (jnp.zeros((), jnp.int32), head_start),
        )
        small_term = (
            bias_full,
            jnp.sum(grad_attn.astype(jnp.float32), axis=0),
            jnp.sum(grad_pre.astype(jnp.float32), axis=0),
            jnp.sum(grad_branch.astype(jnp.float32), axis=0),
            jnp.stack([gain_one, gain_two]),
            jnp.stack([shift_one, shift_two]),
        )
        small_total = accumulate(small_total, small_term)
        token_term = (out_term, in_term, back_term)
        head_total = accumulate(head_total, reduce_heads(head_term))
        token_total = accumulate(token_total, reduce_tokens(token_term))
    small_sums = lax.psum(
        (
            small_total[0],
            small_total[1],
            small_total[2],
            small_total[3],
            small_total[4],
            small_total[5],
        ),
        ("dp", "head"),
    )
    return (
        jnp.stack(outputs),
        jnp.stack(input_grads),
        head_total,
        small_sums[0],
        token_total[0],
        small_sums[1],
        token_total[1],
        small_sums[2],
        token_total[2],
        small_sums[3],
        small_sums[4],
        small_sums[5],
    )


def solution(mesh):
    return jax.shard_map(
        on_device,
        mesh=mesh,
        in_specs=(
            P(None, ("dp", "head"), None),
            P(None, "dp", None),
            P(None, "dp", "head"),
            P(),
            P(None, ("dp", "head")),
            P(),
            P(None, ("dp", "head")),
            P(),
            P(None, ("dp", "head")),
            P(),
            P(),
            P(),
            P(None, ("dp", "head"), None),
        ),
        out_specs=(
            P(None, ("dp", "head"), None),
            P(None, ("dp", "head"), None),
            P(None, "dp", "head"),
            P(),
            P(None, ("dp", "head")),
            P(),
            P(None, ("dp", "head")),
            P(),
            P(None, ("dp", "head")),
            P(),
            P(),
            P(),
        ),
        check_vma=False,
    )
```

profile of v0, /device:TPU:0, one launch (start us, length us, event | category | flops | bytes accessed | tf_op | source)
XLA Modules:
  0.0 1031.0 jit_solution(9810883486489578737)
XLA Ops:
  14.0 26.0 %all-gather.19.cloned.1.call-done = bf16[1,1024,768]{2,1,0:T(8,128)(2,1)} async-done(((bf16[1,512,768]{2,1,0:T(8,128)(2,1)}), bf16[1,1024,768]{2,1,0:T(8,128)(2,1)}) %all-gather.19.cloned.1.call-update) | async-done | bytes 1572880 | tf_op jit(solution)/shard_map/all_gather | solution.py:132
  40.1 42.8 %all-gather.9.cloned.1.call-done = bf16[3,768,384]{2,1,0:T(8,128)(2,1)} async-done(((bf16[3,48,384]{2,1,0:T(8,128)(2,1)}), bf16[3,768,384]{2,1,0:T(8,128)(2,1)}) %all-gather.9.cloned.1.call-update) | async-done | bytes 1769488 | tf_op jit(solution)/shard_map/all_gather | solution.py:72
  88.1 22.8 %all-gather.17.cloned.1.call-done = bf16[1,1024,768]{2,1,0:T(8,128)(2,1)} async-done(((bf16[1,512,768]{2,1,0:T(8,128)(2,1)}), bf16[1,1024,768]{2,1,0:T(8,128)(2,1)}) %all-gather.17.cloned.1.call-update) | async-done | bytes 1572880 | tf_op jit(solution)/shard_map/all_gather | solution.py:132
  130.5 4.8 fusion.149
  136.3 11.5 %while.53 = (s32[]{:T(128)}, bf16[2,512,6,64]{1,3,2,0:T(8,128)(2,1)}, f32[2,6,512]{2,1,0:T(8,128)S(1)}, bf16[2,512,6,64]{1,3,2,0:T(8,128)(2,1)S(1)}, s32[2,512]{...) while((s32[]{:T(128)}, ...), condition=%wide.region_11.12_spmd, body=%wide.region_8.11_spmd.sunk | while | flops 421983232 | bytes 21622876 | solution.py:140
  157.6 11.3 %while.52 = (s32[]{:T(128)}, bf16[2,512,6,64]{1,3,2,0:T(8,128)(2,1)}, f32[2,6,512]{2,1,0:T(8,128)S(1)}, bf16[2,512,6,64]{1,3,2,0:T(8,128)(2,1)}, s32[2,512]{1,0:...) while((s32[]{:T(128)}, ...), condition=%wide.region_3.4_spmd, body=%wide.region_0.3_spmd.sunk | while | flops 421983232 | bytes 31060144 | solution.py:140
  176.3 8.2 all-to-all-done
  188.7 46.1 %all-gather.13.cloned.1.call-done = bf16[768,3072]{0,1:T(8,128)(2,1)} async-done(((bf16[768,96]{0,1:T(8,128)(2,1)}), bf16[768,3072]{0,1:T(8,128)(2,1)}) %all-gather.13.cloned.1.call-update) | async-done | bytes 4718608 | tf_op jit(solution)/shard_map/all_gather | solution.py:75
  234.8 5.3 fusion.165
  242.7 35.5 %multiply_convert_fusion.3 = (bf16[512,3072]{1,0:T(8,128)(2,1)}, f32[512,3072]{1,0:T(8,128)}, bf16[512,3072]{1,0:T(8,128)(2,1)}, f32[512,3072]{1,0:T(8,128)}, f32[512,3072]{1,0:T(8,128)}) fusion(f32[3072]{0:T(1024)S(1)} %copy-done.108, f32[512,3072]{1,0:T(8,128)S(1)} %fusion.165, bf16[768,3072]{0,1:T(8,128)(2,1)S(1)} %copy-done.104, ...), kind=kOutput, calls=%fused_computation.153 | convolution fusion | flops 2625503232 | bytes 37771264 | tf_op jit(solution)/shard_map/dot_general | solution.py:147
  278.2 21.2 %all-gather.15.cloned.1.call-done = bf16[3072,768]{0,1:T(8,128)(2,1)} async-done(((bf16[3072,24]{0,1:T(8,128)(2,1)}), bf16[3072,768]{0,1:T(8,128)(2,1)}) %all-gather.15.cloned.1.call-update) | async-done | bytes 4718608 | tf_op jit(solution)/shard_map/all_gather | solution.py:76
  299.5 6.2 fusion.183
  319.2 17.3 %convert_reduce_fusion.1 = (f32[3072]{0:T(1024)}, bf16[512,3072]{1,0:T(8,128)(2,1)}, f32[3072]{0:T(1024)}, bf16[512,3072]{1,0:T(8,128)(2,1)}) fusion(f32[512,3072]{1,0:T(8,128)} %get-tuple-element.505, f32[512,3072]{1,0:T(8,128)} %get-tuple-element.546, f32[3072]{0:T(1024)S(1)} %copy-done.108, f32[512,3072]{1,0:T(8,128)S(1)} %fusion.184, ...), kind=kOutput, calls=%fused_computation.137 | convolution fusion | flops 2469390336 | bytes 43290624 | tf_op jit(solution)/shard_map/td,fd->tf/dot_general | solution.py:158
  336.5 6.5 add_add_fusion.6
  343.0 6.2 multiply_reduce_fusion.3
  363.1 8.9 all-to-all-done.2
  381.6 22.9 %while.54 = (s32[]{:T(128)}, bf16[2,512,6,64]{1,3,2,0:T(8,128)(2,1)}, bf16[2,512,6,64]{1,3,2,0:T(8,128)(2,1)}, bf16[2,512,6,64]{1,3,2,0:T(8,128)(2,1)}, bf16[2,5...) while((s32[]{:T(128)}, ...), condition=%wide.region_22.23_spmd, body=%wide.region_20.22_spmd.sunk | while | flops 1031468032 | bytes 68001024 | solution.py:175
  409.9 23.3 %while.55 = (s32[]{:T(128)}, bf16[2,512,6,64]{1,3,2,0:T(8,128)(2,1)}, bf16[2,512,6,64]{1,3,2,0:T(8,128)(2,1)}, bf16[2,512,6,64]{1,3,2,0:T(8,128)(2,1)}, bf16[2,5...) while((s32[]{:T(128)}, ...), condition=%wide.region_30.31_spmd, body=%wide.region_28.30_spmd.sunk | while | flops 1031468032 | bytes 68001024 | solution.py:175
  451.4 4.4 fusion.144
  463.7 4.9 bitcast_convert_fusion.1
  468.6 5.5 bitcast_convert_fusion
  478.9 4.8 fusion.186
  483.8 5.5 convolution_add_fusion
  490.7 4.9 fusion.167
  495.6 5.4 convolution_add_fusion.1
  511.7 42.3 %all-reduce.1 = (f32[2,768]{1,0:T(2,128)}, f32[768]{0:T(1024)}, f32[3072]{0:T(1024)}, f32[768]{0:T(1024)}, f32[2,768]{1,0:T(2,128)}, /*index=5*/f32[2,768]{1,0:T(2,128)}) all-reduce(f32[2,768]{1,0:T(2,128)S(1)} %fusion.155, f32[768]{0:T(1024)S(1)} %add.321, f32[3072]{0:T(1024)S(1)} %add.323, ...), channel_id=1, replica_groups=mesh['dp'=16,'head'=2] {'dp','head'}, use_global_device_ids=true, to_apply=%region_38.39 | all-reduce | flops 9216 | bytes 73728 | tf_op jit(solution)/shard_map/psum | solution.py:221
  554.1 25.0 %all-reduce.4.cloned.1.call-done = f32[3,768,384]{2,0,1:T(4,128)} async-done(((f32[3,768,384]{2,0,1:T(4,128)}), f32[3,768,384]{2,0,1:T(4,128)}) %all-reduce.4.cloned.1.call-update) | async-done | bytes 3538960
  580.8 26.1 %reduce-scatter.6.cloned.1.call-done = bf16[512,768]{1,0:T(8,128)(2,1)} async-done(((bf16[1024,768]{1,0:T(8,128)(2,1)}), bf16[512,768]{1,0:T(8,128)(2,1)}) %reduce-scatter.6.cloned.1.call-update) | async-done | bytes 786448 | tf_op jit(solution)/shard_map/reduce_scatter | solution.py:189
  609.4 26.0 %reduce-scatter.8.cloned.1.call-done = bf16[512,768]{1,0:T(8,128)(2,1)} async-done(((bf16[1024,768]{1,0:T(8,128)(2,1)}), bf16[512,768]{1,0:T(8,128)(2,1)}) %reduce-scatter.8.cloned.1.call-update) | async-done | bytes 786448 | tf_op jit(solution)/shard_map/reduce_scatter | solution.py:189
  638.7 102.0 %reduce-scatter.10.cloned.1.call-done = f32[768,24]{0,1:T(8,128)} async-done(((f32[768,768]{0,1:T(8,128)}), f32[768,24]{0,1:T(8,128)}) %reduce-scatter.10.cloned.1.call-update) | async-done | bytes 73744 | tf_op jit(solution)/shard_map/reduce_scatter | solution.py:87
  740.8 141.7 %reduce-scatter.14.cloned.1.call-done = f32[3072,24]{0,1:T(8,128)} async-done(((f32[3072,768]{0,1:T(8,128)}), f32[3072,24]{0,1:T(8,128)}) %reduce-scatter.14.cloned.1.call-update) | async-done | bytes 294928 | tf_op jit(solution)/shard_map/reduce_scatter | solution.py:89
  882.4 141.5 %reduce-scatter.12.cloned.1.call-done = f32[768,96]{0,1:T(8,128)} async-done(((f32[768,3072]{0,1:T(8,128)}), f32[768,96]{0,1:T(8,128)}) %reduce-scatter.12.cloned.1.call-update) | async-done | bytes 294928 | tf_op jit(solution)/shard_map/reduce_scatter | solution.py:88
  (468 shorter events, 215.5 us)
Async XLA Ops:
  7.2 32.9 %all-gather.19.cloned.1.call-start = ((), (), s32[]{:S(2)}) async-start(), calls=%async_computation.16 | async-start | bytes 2359296 | tf_op jit(solution)/shard_map/all_gather | solution.py:132
  9.9 73.0 %all-gather.9.cloned.1.call-start = ((), (), s32[]{:S(2)}) async-start(), calls=%async_computation.9 | async-start | bytes 1880064 | tf_op jit(solution)/shard_map/all_gather | solution.py:72
  10.7 100.2 %all-gather.17.cloned.1.call-start = ((), (), s32[]{:S(2)}) async-start(), calls=%async_computation.15 | async-start | bytes 2359296 | tf_op jit(solution)/shard_map/all_gather | solution.py:132
  11.4 161.1 %all-gather.11.cloned.1.call-start = ((), (), s32[]{:S(2)}) async-start(), calls=%async_computation.10 | async-start | bytes 1216512 | tf_op jit(solution)/shard_map/all_gather | solution.py:74
  12.0 222.8 %all-gather.13.cloned.1.call-start = ((), (), s32[]{:S(2)}) async-start(), calls=%async_computation.11 | async-start | bytes 4866048 | tf_op jit(solution)/shard_map/all_gather | solution.py:75
  12.6 286.9 %all-gather.15.cloned.1.call-start = ((), (), s32[]{:S(2)}) async-start(), calls=%async_computation.12 | async-start | bytes 4866048 | tf_op jit(solution)/shard_map/all_gather | solution.py:76
  14.0 292.0 %copy-start.72 = (f32[768]{0:T(1024)}, f32[768]{0:T(1024)S(1)}, u32[]{:S(2)}) copy-start(f32[768]{0:T(1024)S(1)} %get-tuple-element.407) | copy-start | bytes 9220
  14.0 335.3 %copy-start.70 = (f32[768]{0:T(1024)}, f32[768]{0:T(1024)S(1)}, u32[]{:S(2)}) copy-start(f32[768]{0:T(1024)S(1)} %get-tuple-element.554) | copy-start | bytes 9220
  147.8 21.2 %all-to-all-start.1 = ((bf16[2,512,384]{1,2,0:T(8,128)(2,1)}), bf16[2,512,384]{1,2,0:T(8,128)(2,1)}, u32[]{:S(2)}, u32[]{:S(2)}) async-start(bf16[2,512,384]{1,2,0:T(8,128)(2,1)} %bitcast.52), calls=%async_computation.1 | async-start | bytes 1572864 | tf_op jit(solution)/shard_map/all_to_all | solution.py:142
  168.9 15.5 %all-to-all-start = ((bf16[2,512,384]{1,2,0:T(8,128)(2,1)}), bf16[2,512,384]{1,2,0:T(8,128)(2,1)S(1)}, u32[]{:S(2)}, u32[]{:S(2)}) async-start(bf16[2,512,384]{1,2,0:T(8,128)(2,1)} %bitcast.373), calls=%async_computation | async-start | bytes 1572864 | tf_op jit(solution)/shard_map/all_to_all | solution.py:142
  176.3 173.0 %copy-start.74 = (f32[512]{0:T(512)}, f32[512]{0:T(512)S(1)}, u32[]{:S(2)}) copy-start(f32[512]{0:T(512)S(1)} %broadcast_multiply_fusion.1) | copy-start | bytes 6148
  188.0 155.0 %copy-start.33 = (f32[512,768]{1,0:T(8,128)}, f32[512,768]{1,0:T(8,128)S(1)}, u32[]{:S(2)}) copy-start(f32[512,768]{1,0:T(8,128)S(1)} %get-tuple-element.543) | copy-start | bytes 4718596
  188.0 161.3 %copy-start.83 = (f32[512]{0:T(512)}, f32[512]{0:T(512)S(1)}, u32[]{:S(2)}) copy-start(f32[512]{0:T(512)S(1)} %broadcast_multiply_fusion.3) | copy-start | bytes 6148
  188.6 160.7 %copy-start.77 = (f32[512]{0:T(512)}, f32[512]{0:T(512)S(1)}, u32[]{:S(2)}) copy-start(f32[512]{0:T(512)S(1)} %fusion.158) | copy-start | bytes 6148
  188.7 160.7 %copy-start.94 = (f32[512]{0:T(512)}, f32[512]{0:T(512)S(1)}, u32[]{:S(2)}) copy-start(f32[512]{0:T(512)S(1)} %fusion.156) | copy-start | bytes 6148
  242.7 56.7 %copy-start.110 = (f32[768]{0:T(1024)S(1)}, f32[768]{0:T(1024)}, u32[]{:S(2)}) copy-start(f32[768]{0:T(1024)} %param.30) | copy-start | bytes 9220
  352.3 26.5 %copy-start.79 = (f32[512]{0:T(512)}, f32[512]{0:T(512)S(1)}, u32[]{:S(2)}) copy-start(f32[512]{0:T(512)S(1)} %negate_multiply_fusion.2) | copy-start | bytes 6148
  356.1 15.9 %all-to-all-start.2 = ((bf16[512,2,384]{2,0,1:T(8,128)(2,1)}), bf16[512,2,384]{2,0,1:T(8,128)(2,1)}, u32[]{:S(2)}, u32[]{:S(2)}) async-start(bf16[512,2,384]{2,0,1:T(8,128)(2,1)} %bitcast.290), calls=%async_computation.2 | async-start | bytes 1572864 | tf_op jit(solution)/shard_map/all_to_all | solution.py:174
  363.1 18.5 %copy-start.65 = (f32[2,6,512]{2,1,0:T(8,128)S(1)}, f32[2,6,512]{2,1,0:T(8,128)}, u32[]{:S(2)}) copy-start(f32[2,6,512]{2,1,0:T(8,128)} %copy-done.64) | copy-start | bytes 73732
  363.1 18.5 %copy-start.69 = (s32[2,512]{1,0:T(2,128)S(1)}, s32[2,512]{1,0:T(2,128)}, u32[]{:S(2)}) copy-start(s32[2,512]{1,0:T(2,128)} %copy-done.68) | copy-start | bytes 12292
  372.0 32.6 %all-to-all-start.3 = ((bf16[512,2,384]{2,0,1:T(8,128)(2,1)}), bf16[512,2,384]{2,0,1:T(8,128)(2,1)}, u32[]{:S(2)}, u32[]{:S(2)}) async-start(bf16[512,2,384]{2,0,1:T(8,128)(2,1)} %bitcast.289), calls=%async_computation.4 | async-start | bytes 1572864 | tf_op jit(solution)/shard_map/all_to_all | solution.py:174
  376.3 202.8 %all-reduce.4.cloned.1.call-start = ((), (), s32[]{:S(2)}) async-start(), calls=%async_computation.20 | async-start | bytes 9437184
  462.1 144.8 %reduce-scatter.6.cloned.1.call-start = ((), (), s32[]{:S(2)}) async-start(), calls=%async_computation.13 | async-start | bytes 2359296 | tf_op jit(solution)/shard_map/reduce_scatter | solution.py:189
  468.6 166.8 %reduce-scatter.8.cloned.1.call-start = ((), (), s32[]{:S(2)}) async-start(), calls=%async_computation.14 | async-start | bytes 2359296 | tf_op jit(solution)/shard_map/reduce_scatter | solution.py:189
  474.1 266.6 %reduce-scatter.10.cloned.1.call-start = ((), (), s32[]{:S(2)}) async-start(), calls=%async_computation.17 | async-start | bytes 2433024 | tf_op jit(solution)/shard_map/reduce_scatter | solution.py:87
  478.8 403.6 %reduce-scatter.14.cloned.1.call-start = ((), (), s32[]{:S(2)}) async-start(), calls=%async_computation.19 | async-start | bytes 9732096 | tf_op jit(solution)/shard_map/reduce_scatter | solution.py:89
  489.3 534.6 %reduce-scatter.12.cloned.1.call-start = ((), (), s32[]{:S(2)}) async-start(), calls=%async_computation.18 | async-start | bytes 9732096 | tf_op jit(solution)/shard_map/reduce_scatter | solution.py:88
  504.2 102.7 %copy-start.11 = (f32[512,768]{1,0:T(8,128)S(1)}, f32[512,768]{1,0:T(8,128)}, u32[]{:S(2)}) copy-start(f32[512,768]{1,0:T(8,128)} %copy-done.10) | copy-start | bytes 4718596
  504.2 102.7 %copy-start.82 = (f32[512]{0:T(512)S(1)}, f32[512]{0:T(512)}, u32[]{:S(2)}) copy-start(f32[512]{0:T(512)} %copy-done.81) | copy-start | bytes 6148
  510.1 125.2 %copy-start.9 = (f32[512,768]{1,0:T(8,128)S(1)}, f32[512,768]{1,0:T(8,128)}, u32[]{:S(2)}) copy-start(f32[512,768]{1,0:T(8,128)} %copy-done.8) | copy-start | bytes 4718596
  510.1 125.2 %copy-start.80 = (f32[512]{0:T(512)S(1)}, f32[512]{0:T(512)}, u32[]{:S(2)}) copy-start(f32[512]{0:T(512)} %copy-done.79) | copy-start | bytes 6148
  609.4 27.3 %copy-start.32 = (f32[1,512,768]{2,1,0:T(8,128)S(1)}, f32[1,512,768]{2,1,0:T(8,128)}, u32[]{:S(2)}) copy-start(f32[1,512,768]{2,1,0:T(8,128)} %add_bitcast_fusion.2) | copy-start | bytes 4718596
  (112 other events, 481.0 us)
Sparse Core Ops, SparseCore 0:
  10.1 29.8 all-gather.18
  42.4 40.4 all-gather.8
  85.0 25.8 all-gather.16
  113.7 55.4 all-gather.10
  171.9 62.8 all-gather.12
  237.6 61.8 all-gather.14
  462.2 116.8 all-reduce.3
  581.4 25.4 reduce-scatter.5
  609.1 26.1 reduce-scatter.7
  641.1 99.6 reduce-scatter.9
  747.2 135.1 reduce-scatter.13
  888.7 135.1 reduce-scatter.11
where the time goes:
time: 1040 us; the launch traced here: 1030 us
  waiting for transfers between devices  641 us (62%)
  matrix products  187 us (18%)
  local copies, waits for them, and re-layouts  78.7 us (8%)
  other arithmetic  46.1 us (4%)
  blocking collectives  42.3 us (4%)
  starting transfers between devices  17.2 us (2%)
  between operations  16.5 us (2%)
    reduce_scatter x1, waiting for transfers between devices, reduce_tokens(): lax.psum_scatter(token_terms[2], ('dp', 'head'), scatter_dimension=1, til...  142 us
    reduce_scatter x1, waiting for transfers between devices, reduce_tokens(): lax.psum_scatter(token_terms[1], ('dp', 'head'), scatter_dimension=1, til...  142 us
    reduce_scatter x1, waiting for transfers between devices, reduce_tokens(): lax.psum_scatter(token_terms[0], ('dp', 'head'), scatter_dimension=1, til...  102 us
    reduce_scatter x2, waiting for transfers between devices, on_device(): lax.psum_scatter(jnp.einsum('ctf,cdf->td', grad_proj, head_full, preferre...  52 us
    all_gather x2, waiting for transfers between devices, on_device(): x_group = lax.all_gather(x_local, 'head', axis=0, tiled=True)  48.8 us
    all_gather x1, waiting for transfers between devices, fetch_weights(): lax.all_gather(w_in, ('dp', 'head'), axis=1, tiled=True)  46.1 us
    all_gather x1, waiting for transfers between devices, fetch_weights(): head_full = lax.all_gather(w_qkv, 'dp', axis=1, tiled=True)  42.8 us
    psum x1, blocking collectives, on_device(): lax.psum((small_total[0], small_total[1], small_total[2], small_total[3],...  42.3 us
  transfers between devices with their start and end apart: 16, of which 13 were waited for; matrix products, arithmetic and copies ran while one was open for 18% of the time, Pallas kernels for 0%

commit v1 on v0

v1 whole, which is shorter than its diff:
```python
import functools
import math

import jax
import jax.numpy as jnp
from jax import lax
from jax.experimental import pallas as pl
from jax.experimental.pallas import tpu as pltpu
from jax.sharding import PartitionSpec as P

HD = 64
NORM_EPS = 1e-05
MASKED = -1e30
AXES = ("dp", "head")
F32 = jnp.float32
BF16 = jnp.bfloat16


def dot(left, right, left_dim, right_dim):
    return lax.dot_general(
        left, right, (((left_dim,), (right_dim,)), ((), ())), preferred_element_type=F32
    )


def fill_mask(segment_row, segment_col, mask_ref):
    @pl.when(pl.program_id(1) == 0)
    def _():
        mask_ref[...] = jnp.where(segment_col[0] == segment_row[0], 0.0, MASKED)


def lane_halves(rows):
    lane = lax.broadcasted_iota(jnp.int32, (rows, 2 * HD), 1)
    return lane < HD


def attend_kernel(seg_row, seg_col, qkv_ref, context_ref, total_ref, mask_ref):
    fill_mask(seg_row, seg_col, mask_ref)
    queries = qkv_ref[0] * jnp.asarray(HD**-0.5, BF16)
    key_rows = qkv_ref[1]
    values = qkv_ref[2]
    first = lane_halves(key_rows.shape[0])
    parts = []
    for head in range(2):
        keys_own = jnp.where(first if head == 0 else ~first, key_rows, jnp.zeros_like(key_rows))
        scores = dot(keys_own, queries, 1, 1) + mask_ref[...]
        highest = jnp.max(scores, axis=0, keepdims=True)
        exponent = jnp.exp(scores - highest)
        totals = jnp.sum(exponent, axis=0, keepdims=True)
        low = (exponent * (1.0 / totals)).astype(BF16)
        total_ref[0, 0, head : head + 1, :] = highest + jnp.log(totals)
        parts.append(dot(values, low, 0, 0))
    joined = jnp.concatenate([parts[0][:HD], parts[1][HD:]], axis=0)
    context_ref[...] = joined.T.astype(BF16)


def attend_back_kernel(seg_row, seg_col, qkv_ref, total_ref, grad_ref, out_ref, mask_ref):
    fill_mask(seg_row, seg_col, mask_ref)
    scale = jnp.asarray(HD**-0.5, BF16)
    queries = qkv_ref[0] * scale
    key_rows = qkv_ref[1]
    key_scaled = key_rows * scale
    values = qkv_ref[2]
    grad = grad_ref[...]
    first = lane_halves(key_rows.shape[0])
    grad_queries, grad_keys, grad_values = [], [], []
    for head in range(2):
        own = first if head == 0 else ~first
        zero = jnp.zeros_like(key_rows)
        scores = dot(jnp.where(own, key_rows, zero), queries, 1, 1) + mask_ref[...]
        probs = jnp.exp(scores - total_ref[0, 0, head : head + 1, :])
        grad_probs = dot(jnp.where(own, values, zero), grad, 1, 1)
        weighted = jnp.sum(probs * grad_probs, axis=0, keepdims=True)
        grad_scores = (probs * (grad_probs - weighted)).astype(BF16)
        grad_values.append(dot(probs.astype(BF16), grad, 1, 0))
        grad_keys.append(dot(grad_scores, queries, 1, 0))
        grad_queries.append(dot(key_scaled, grad_scores, 0, 0))
    joined = jnp.concatenate([grad_queries[0][:HD], grad_queries[1][HD:]], axis=0)
    out_ref[0] = joined.T.astype(BF16)
    out_ref[1] = jnp.where(first, grad_keys[0], grad_keys[1]).astype(BF16)
    out_ref[2] = jnp.where(first, grad_values[0], grad_values[1]).astype(BF16)


def attention_specs(seq_len):
    return dict(
        row=pl.BlockSpec((1, 1, seq_len), lambda r, h: (r, 0, 0)),
        col=pl.BlockSpec((1, seq_len, 1), lambda r, h: (r, 0, 0)),
        three=pl.BlockSpec((3, seq_len, 2 * HD), lambda r, h: (0, r, h)),
        one=pl.BlockSpec((seq_len, 2 * HD), lambda r, h: (r, h)),
        total=pl.BlockSpec((1, 1, 8, seq_len), lambda r, h: (r, h, 0, 0)),
    )


def attend(segments, qkv):
    rows, seq_len = segments.shape
    pairs = qkv.shape[2] // (2 * HD)
    s = attention_specs(seq_len)
    area = rows * pairs * 2 * seq_len * seq_len
    return pl.pallas_call(
        attend_kernel,
        grid=(rows, pairs),
        in_specs=[s["row"], s["col"], s["three"]],
        out_specs=[s["one"], s["total"]],
        out_shape=[
            jax.ShapeDtypeStruct(qkv.shape[1:], BF16),
            jax.ShapeDtypeStruct((rows, pairs, 8, seq_len), F32),
        ],
        scratch_shapes=[pltpu.VMEM((seq_len, seq_len), F32)],
        cost_estimate=pl.CostEstimate(
            flops=area * 512, bytes_accessed=qkv.size * 3, transcendentals=area
        ),
        name="attend",
    )(segments[:, None, :], segments[:, :, None], qkv)


def attend_back(segments, qkv, totals, grad):
    rows, seq_len = segments.shape
    pairs = qkv.shape[2] // (2 * HD)
    s = attention_specs(seq_len)
    area = rows * pairs * 2 * seq_len * seq_len
    return pl.pallas_call(
        attend_back_kernel,
        grid=(rows, pairs),
        in_specs=[s["row"], s["col"], s["three"], s["total"], s["one"]],
        out_specs=s["three"],
        out_shape=jax.ShapeDtypeStruct(qkv.shape, BF16),
        scratch_shapes=[pltpu.VMEM((seq_len, seq_len), F32)],
        cost_estimate=pl.CostEstimate(
            flops=area * 1280, bytes_accessed=qkv.size * 5, transcendentals=area
        ),
        name="attend_back",
    )(segments[:, None, :], segments[:, :, None], qkv, totals, grad)


def gelu_parts(value):
    size = jnp.abs(value)
    bell = jnp.exp(-0.5 * value * value)
    t = 1.0 / (1.0 + (0.3275911 / math.sqrt(2.0)) * size)
    series = 1.061405429 / 2
    for factor in (-1.453152027 / 2, 1.421413741 / 2, -0.284496736 / 2, 0.254829592 / 2):
        series = series * t + factor
    tail = series * t * bell
    cumulative = jnp.where(value < 0, tail, 1.0 - tail)
    return cumulative, value * bell * (1.0 / math.sqrt(2.0 * math.pi))


def norm_stats(residual):
    average = jnp.mean(residual, axis=-1, keepdims=True)
    centred = residual - average
    spread = jnp.mean(centred * centred, axis=-1, keepdims=True)
    inverse = lax.rsqrt(spread + NORM_EPS)
    return centred * inverse, inverse


def norm_back(normal, inverse, grad, gain):
    weighted = grad * gain
    along = jnp.mean(weighted * normal, axis=-1, keepdims=True)
    return inverse * (weighted - jnp.mean(weighted, axis=-1, keepdims=True) - normal * along)


def gather(shard):
    return lax.all_gather(shard, AXES, axis=0, tiled=True)


def reduce_rows(term):
    return lax.psum_scatter(term.astype(BF16), AXES, scatter_dimension=0, tiled=True)


def on_device(
    tokens,
    segment_ids,
    w_qkv,
    qv_bias,
    w_out,
    out_bias,
    w_in,
    in_bias,
    w_back,
    back_bias,
    norm_gains,
    norm_shifts,
    out_cotangent,
    *,
    dp_size,
    head_size,
):
    micro, local, width = tokens.shape
    seq_len = segment_ids.shape[2]
    own_rows = local // seq_len
    part, own_width = w_qkv.shape[1], w_qkv.shape[2]
    shard = (3, part, own_width)

    gathered = lax.all_gather(w_qkv.reshape(3 * part, own_width), AXES, axis=0, tiled=True)
    qkv_full = (
        gathered.reshape((dp_size, head_size) + shard)
        .transpose(2, 0, 3, 1, 4)
        .reshape(3, dp_size * part, head_size * own_width)
    )
    out_full = gather(w_out.T)
    in_full = gather(w_in.T)
    back_full = gather(w_back.T)

    x = tokens.reshape(micro * local, width)
    segments = lax.dynamic_slice_in_dim(
        segment_ids, lax.axis_index("head") * own_rows, own_rows, 1
    ).reshape(micro * own_rows, seq_len)
    bias = jnp.stack([qv_bias[0], jnp.zeros_like(qv_bias[0]), qv_bias[1]])[:, None, :]
    qkv = (
        jnp.einsum("td,cdf->ctf", x, qkv_full, preferred_element_type=F32) + bias
    ).astype(BF16)
    context, totals = attend(segments, qkv)
    attended = dot(context, out_full, 1, 1) + out_bias
    normal_one, inverse_one = norm_stats(x.astype(F32) + attended)
    hidden = normal_one * norm_gains[0] + norm_shifts[0]
    hidden_low = hidden.astype(BF16)
    pre_act = dot(hidden_low, in_full, 1, 1) + in_bias
    cumulative, along = gelu_parts(pre_act)
    activation = (pre_act * cumulative).astype(BF16)
    slope = cumulative + along
    branch = dot(activation, back_full, 1, 1) + back_bias
    normal_two, inverse_two = norm_stats(hidden + branch)
    out = (normal_two * norm_gains[1] + norm_shifts[1]).astype(BF16)

    error = out_cotangent.reshape(micro * local, width).astype(F32)
    grad_two = norm_back(normal_two, inverse_two, error, norm_gains[1])
    gain_two = jnp.sum(error * normal_two, axis=0)
    shift_two = jnp.sum(error, axis=0)
    grad_branch = grad_two.astype(BF16)
    back_grad = reduce_rows(dot(grad_branch, activation, 0, 0))
    grad_pre = (slope * dot(grad_branch, back_full, 1, 0)).astype(BF16)
    in_grad = reduce_rows(dot(grad_pre, hidden_low, 0, 0))
    grad_hidden = grad_two + dot(grad_pre, in_full, 1, 0)
    grad_one = norm_back(normal_one, inverse_one, grad_hidden, norm_gains[0])
    gain_one = jnp.sum(grad_hidden * normal_one, axis=0)
    shift_one = jnp.sum(grad_hidden, axis=0)
    grad_attn = grad_one.astype(BF16)
    out_grad = reduce_rows(dot(grad_attn, context, 0, 0))
    grad_context = dot(grad_attn, out_full, 1, 0).astype(BF16)
    grad_qkv = attend_back(segments, qkv, totals, grad_context)
    term = jnp.einsum("td,ctf->cdf", x, grad_qkv, preferred_element_type=F32)
    term = (
        term.astype(BF16)
        .reshape(3, dp_size, part, head_size, own_width)
        .transpose(1, 3, 0, 2, 4)
        .reshape(dp_size * head_size * 3 * part, own_width)
    )
    qkv_grad = lax.psum_scatter(term, AXES, scatter_dimension=0, tiled=True)
    x_grad = grad_one + jnp.einsum(
        "ctf,cdf->td", grad_qkv, qkv_full, preferred_element_type=F32
    )
    small = jnp.concatenate(
        [
            jnp.sum(grad_qkv[0].astype(F32), axis=0),
            jnp.sum(grad_qkv[2].astype(F32), axis=0),
            jnp.sum(grad_attn.astype(F32), axis=0),
            jnp.sum(grad_pre.astype(F32), axis=0),
            jnp.sum(grad_branch.astype(F32), axis=0),
            gain_one,
            gain_two,
            shift_one,
            shift_two,
        ]
    )
    small = lax.psum(small, AXES)
    hidden_width = in_bias.shape[0]
    cuts, at = [], 0
    for size in (2 * width, width, hidden_width, width, 2 * width, 2 * width):
        cuts.append(small[at : at + size])
        at += size
    return (
        out.reshape(tokens.shape),
        x_grad.reshape(tokens.shape),
        qkv_grad.astype(F32).reshape(shard),
        cuts[0].reshape(2, width),
        out_grad.astype(F32).T,
        cuts[1],
        in_grad.astype(F32).T,
        cuts[2],
        back_grad.astype(F32).T,
        cuts[3],
        cuts[4].reshape(2, width),
        cuts[5].reshape(2, width),
    )


def solution(mesh):
    return jax.shard_map(
        functools.partial(
            on_device, dp_size=mesh.shape["dp"], head_size=mesh.shape["head"]
        ),
        mesh=mesh,
        in_specs=(
            P(None, AXES, None),
            P(None, "dp", None),
            P(None, "dp", "head"),
            P(),
            P(None, AXES),
            P(),
            P(None, AXES),
            P(),
            P(None, AXES),
            P(),
            P(),
            P(),
            P(None, AXES, None),
        ),
        out_specs=(
            P(None, AXES, None),
            P(None, AXES, None),
            P(None, "dp", "head"),
            P(),
            P(None, AXES),
            P(),
            P(None, AXES),
            P(),
            P(None, AXES),
            P(),
            P(),
            P(),
        ),
        check_vma=False,
    )
```

time: 1040 us -> 751 us (0.72)
  waiting for transfers between devices: 641 us -> 466 us
  matrix products: 187 us -> 111 us
  Pallas kernels: 0 us -> 43.5 us
  local copies, waits for them, and re-layouts: 78.7 us -> 51.1 us
  other arithmetic: 46.1 us -> 19.1 us
  starting transfers between devices: 17.2 us -> 0.32 us
    reduce_scatter x5 -> x4, waiting for transfers between devices: 437 us -> 281 us  [the longest x3 221 us: reduce_rows(): lax.psum_scatter(term.astype(BF16), AXES, scatter_dimension=0, tiled=True)]
    dot_general x52 -> x12, matrix products: 187 us -> 111 us  [the longest x9 86.9 us: dot(): lax.dot_general(left, right, (((left_dim,), (right_dim,)), ((), ())), pre...]
    pallas_call x0 -> x2, Pallas kernels: none -> 43.5 us  [the longest x1 24.9 us: attend_back(): pl.pallas_call(attend_back_kernel, grid=(rows, pairs), in_specs=[s['row']...]
    unnamed x13 -> x8, waiting for transfers between devices: 28.1 us -> 2.65 us
    all_gather x6 -> x4, waiting for transfers between devices: 159 us -> 182 us  [the longest x3 127 us: gather(): return lax.all_gather(shard, AXES, axis=0, tiled=True)]
    all_to_all x4 -> x0, waiting for transfers between devices: 17.1 us -> none  [the longest x2 8.89 us: on_device(): lax.all_to_all(grad_ctx, 'head', split_axis=1, concat_axis=0, tiled=True)]
    another operation x27 -> x2, local copies, waits for them, and re-layouts: 17.7 us -> 1.08 us  [the longest x1 1 us: attend(): segments[:, :, None]]
    all_to_all x4 -> x0, starting transfers between devices: 16.5 us -> none  [the longest x2 8.65 us: on_device(): lax.all_to_all(grad_ctx, 'head', split_axis=1, concat_axis=0, tiled=True)]
  transfers between devices with their start and end apart: 16 -> 8, of which waited for: 13 -> 7; matrix products, arithmetic and copies ran while one was open for 18% -> 17% of each run, Pallas kernels for 0% -> 6%
where the time goes in v1:
time: 751 us; the launch traced here: 746 us
  waiting for transfers between devices  466 us (62%)
  matrix products  111 us (15%)
  local copies, waits for them, and re-layouts  51.1 us (7%)
  Pallas kernels  43.5 us (6%)
  blocking collectives  39.8 us (5%)
  other arithmetic  19.1 us (3%)
  between operations  14.8 us (2%)
    reduce_scatter x3, waiting for transfers between devices, reduce_rows(): lax.psum_scatter(term.astype(BF16), AXES, scatter_dimension=0, tiled=True)  221 us
    all_gather x3, waiting for transfers between devices, gather(): return lax.all_gather(shard, AXES, axis=0, tiled=True)  127 us
    dot_general x9, matrix products, dot(): lax.dot_general(left, right, (((left_dim,), (right_dim,)), ((), ())), pre...  86.9 us
    reduce_scatter x1, waiting for transfers between devices, on_device(): qkv_grad = lax.psum_scatter(term, AXES, scatter_dimension=0, tiled=True)  59.7 us
    all_gather x1, waiting for transfers between devices, on_device(): lax.all_gather(w_qkv.reshape(3 * part, own_width), AXES, axis=0, tiled=True)  55.1 us
    psum x1, blocking collectives, on_device(): small = lax.psum(small, AXES)  39.8 us
    pallas_call x1, Pallas kernels, attend_back(): pl.pallas_call(attend_back_kernel, grid=(rows, pairs), in_specs=[s['row']...  24.9 us
    pallas_call x1, Pallas kernels, attend(): pl.pallas_call(attend_kernel, grid=(rows, pairs), in_specs=[s['row'], s['...  18.7 us
  transfers between devices with their start and end apart: 8, of which 7 were waited for; matrix products, arithmetic and copies ran while one was open for 17% of the time, Pallas kernels for 6%

profile of v1, /device:TPU:0, one launch (start us, length us, event | category | flops | bytes accessed | tf_op | source)
XLA Modules:
  0.0 746.0 jit_solution(11124523842009027187)
XLA Ops:
  13.7 2.7 convert_reduce_fusion.1
  18.6 55.1 %all-gather.5.cloned.1.call-done = bf16[4608,384]{1,0:T(8,128)(2,1)} async-done(((bf16[144,384]{1,0:T(8,128)(2,1)}), bf16[4608,384]{1,0:T(8,128)(2,1)}) %all-gather.5.cloned.1.call-update) | async-done | bytes 3538960 | tf_op jit(solution)/shard_map/all_gather | solution.py:192
  73.6 4.9 copy.28
  78.5 4.2 reshape.144
  82.7 8.5 %fusion.7.qkv_ref = bf16[3,1024,768]{2,1,0:T(8,128)(2,1)} fusion(f32[3,768]{1,0:T(4,128)} %pad_maximum_fusion, bf16[1024,768,1]{1,0,2:T(8,128)(2,1)} %bitcast.78, bf16[3,768,768]{2,1,0:T(8,128)(2,1)} %reshape.144), kind=kOutput, calls=%fused_computation.14 | convolution fusion | flops 3628597248 | bytes 9839616 | tf_op jit(solution)/shard_map/td,cdf->ctf/dot_general | solution.py:208
  91.2 18.7 %attend.1 = (bf16[1024,768]{1,0:T(8,128)(2,1)}, f32[2,6,8,512]{3,2,1,0:T(8,128)}) custom-call(s32[2,1,512]{2,1,0:T(1,128)} %get-tuple-element.35.seg_row, s32[2,512,1]{2,1,0:T(8,128)} %broadcast_in_dim_reshape.5.seg_col, bf16[3,1024,768]{2,1,0:T(8,128)(2,1)} %fusion.7.qkv_ref), custom_call_target="tpu_custom_call" | custom-call | flops 3221225472 | bytes 7077888 | tf_op jit(solution)/shard_map/attend/pallas_call | solution.py:98
  109.9 19.6 %all-gather.7.cloned.1.call-done = bf16[768,768]{1,0:T(8,128)(2,1)} async-done(((bf16[24,768]{1,0:T(8,128)(2,1)}), bf16[768,768]{1,0:T(8,128)(2,1)}) %all-gather.7.cloned.1.call-update) | async-done | bytes 1179664 | tf_op jit(solution)/shard_map/all_gather | solution.py:161
  129.5 3.8 fusion.28
  133.8 61.0 %all-gather.9.cloned.1.call-done = bf16[3072,768]{1,0:T(8,128)(2,1)} async-done(((bf16[96,768]{1,0:T(8,128)(2,1)}), bf16[3072,768]{1,0:T(8,128)(2,1)}) %all-gather.9.cloned.1.call-update) | async-done | bytes 4718608 | tf_op jit(solution)/shard_map/all_gather | solution.py:161
  194.8 18.1 %multiply_convert_fusion = (bf16[1024,3072]{1,0:T(8,128)(2,1)}, f32[1024,3072]{1,0:T(8,128)}) fusion(f32[3072]{0:T(1024)S(1)} %copy-done.20, bf16[3072,768]{1,0:T(8,128)(2,1)} %all-gather.9.cloned.1.call-done, f32[1024,768]{1,0:T(8,128)S(1)} %get-tuple-element.45, f32[768]{0:T(1024)S(1)} %copy-done.15, f32[768]{0:T(1024)S(1)} %get-tuple-element.53, ...), kind=kOutput, calls=%fused_computation.10 | convolution fusion | flops 4904976384 | bytes 26765312 | tf_op jit(solution)/shard_map/dot_general | solution.py:20
  212.9 46.6 %all-gather.11.cloned.1.call-done = bf16[768,3072]{1,0:T(8,128)(2,1)} async-done(((bf16[24,3072]{1,0:T(8,128)(2,1)}), bf16[768,3072]{1,0:T(8,128)(2,1)}) %all-gather.11.cloned.1.call-update) | async-done | bytes 4718608 | tf_op jit(solution)/shard_map/all_gather | solution.py:161
  259.5 9.1 %fusion.29 = (f32[1024]{0:T(1024)S(1)}, f32[1024,768]{1,0:T(8,128)S(1)}) fusion(f32[768]{0:T(1024)S(1)} %copy-done.22, bf16[1024,3072]{1,0:T(8,128)(2,1)} %get-tuple-element.46, bf16[768,3072]{1,0:T(8,128)(2,1)} %all-gather.11.cloned.1.call-done, f32[768]{0:T(1024)S(1)} %copy-done.15, f32[768]{0:T(1024)S(1)} %get-tuple-element.53, ...), kind=kOutput, calls=%fused_computation.84 | convolution fusion | flops 4837342208 | bytes 17323008 | tf_op jit(solution)/shard_map/dot_general | solution.py:20
  271.8 2.3 convert_reduce_fusion.2
  274.7 19.8 %convert_reduce_fusion = (f32[3072]{0:T(1024)}, bf16[1024,3072]{1,0:T(8,128)(2,1)}) fusion(bf16[768,3072]{1,0:T(8,128)(2,1)S(1)} %copy-done.17, f32[1024,768]{1,0:T(8,128)S(1)} %get-tuple-element.31, f32[1024,3072]{1,0:T(8,128)} %get-tuple-element.47, f32[3072]{0:T(1024)S(1)} %copy-done.20), kind=kOutput, calls=%fused_computation.9 | convolution fusion | flops 4917556224 | bytes 26763264 | tf_op jit(solution)/shard_map/dot_general | solution.py:20
  294.5 8.8 %multiply_reduce_fusion = (f32[768]{0:T(1024)}, f32[1024]{0:T(1024)S(1)}, f32[1024]{0:T(1024)S(1)}, f32[768]{0:T(1024)}, f32[1024,768]{1,0:T(8,128)S(1)}) fusion(f32[1024,768]{1,0:T(8,128)S(1)} %get-tuple-element.45, f32[1024]{0:T(1024)S(1)} %add_rsqrt_fusion.1, f32[1024]{0:T(1024)S(1)} %broadcast_multiply_fusion.4, f32[768]{0:T(1024)S(1)} %copy-done.9, ...), kind=kOutput, calls=%fused_computation.28 | convolution fusion | flops 4839698432 | bytes 20472832 | tf_op jit(solution)/shard_map/dot_general | solution.py:20
  306.7 2.5 convolution_convert_fusion.3
  309.3 4.4 convolution_convert_fusion.2.grad_ref
  313.8 24.9 %attend_back.1 = bf16[3,1024,768]{2,1,0:T(8,128)(2,1)} custom-call(s32[2,1,512]{2,1,0:T(1,128)} %get-tuple-element.35.seg_row, s32[2,512,1]{2,1,0:T(8,128)} %broadcast_in_dim_reshape.5.seg_col, bf16[3,1024,768]{2,1,0:T(8,128)(2,1)} %fusion.7.qkv_ref, f32[2,6,8,512]{3,2,1,0:T(8,128)} %get-tuple-element.15.total_ref, ...), custom_call_target="tpu_custom_call" | custom-call | flops 8053063680 | bytes 11796480 | tf_op jit(solution)/shard_map/attend_back/pallas_call | solution.py:120
  338.7 7.8 %convert_bitcast_fusion = bf16[3,768,768]{1,2,0:T(8,128)(2,1)} fusion(bf16[3,1024,768]{2,1,0:T(8,128)(2,1)} %attend_back.1, bf16[1024,768,1]{1,0,2:T(8,128)(2,1)S(1)} %bitcast.80), kind=kOutput, calls=%fused_computation.15 | convolution fusion | flops 3625648128 | bytes 9830400 | tf_op jit(solution)/shard_map/td,ctf->cdf/dot_general | solution.py:239
  346.5 4.3 copy.34
  350.8 3.1 reshape.147
  353.9 4.4 copy.35
  358.4 1.8 copy-done.2
  360.2 10.7 %convolution_convert_fusion.1 = bf16[3072,768]{1,0:T(8,128)(2,1)} fusion(bf16[1024,3072]{1,0:T(8,128)(2,1)} %get-tuple-element.52, f32[1024,768]{1,0:T(8,128)S(1)} %copy-done.2, f32[768]{0:T(1024)S(1)} %copy-done.16, f32[768]{0:T(1024)S(1)} %copy-done.9, f32[1024]{0:T(1024)S(1)} %copy-done.12, f32[1024]{0:T(1024)S(1)} %broadcast_multiply_fusion.4), kind=kOutput, calls=%fused_computation.13 | convolution fusion | flops 4838129664 | bytes 14170112 | tf_op jit(solution)/shard_map/dot_general | solution.py:20
  371.0 1.8 copy-done.5
  372.8 9.7 %convolution_convert_fusion = bf16[768,3072]{1,0:T(8,128)(2,1)} fusion(bf16[1024,3072]{1,0:T(8,128)(2,1)} %get-tuple-element.46, f32[1024,768]{1,0:T(8,128)S(1)} %copy-done.5), kind=kOutput, calls=%fused_computation.12 | convolution fusion | flops 4834983936 | bytes 14155776 | tf_op jit(solution)/shard_map/dot_general | solution.py:20
  382.6 2.5 convert_reduce_fusion.4
  396.8 39.8 %psum.7 = f32[9216]{0:T(1024)} all-reduce(f32[9216]{0:T(1024)} %constant_dynamic-update-slice_fusion), channel_id=1, replica_groups=mesh['dp'=16,'head'=2] {'dp','head'}, use_global_device_ids=true, to_apply=%region_18.19 | all-reduce | flops 9216 | bytes 73728 | tf_op jit(solution)/shard_map/psum | solution.py:263
  443.2 8.2 %bitcast_add_fusion = f32[1024,768]{1,0:T(8,128)} fusion(f32[1024,768]{1,0:T(8,128)} %copy-done.6, bf16[3,1024,768]{2,1,0:T(8,128)(2,1)} %attend_back.1, bf16[3,768,768]{2,1,0:T(8,128)(2,1)S(1)} %copy-done.3), kind=kOutput, calls=%fused_computation.16 | convolution fusion | flops 3624665088 | bytes 14548992 | tf_op jit(solution)/shard_map/ctf,cdf->td/dot_general | solution.py:247
  452.8 59.7 %reduce-scatter.5.cloned.1.call-done = bf16[144,384]{1,0:T(8,128)(2,1)} async-done(((bf16[4608,384]{1,0:T(8,128)(2,1)}), bf16[144,384]{1,0:T(8,128)(2,1)}) %reduce-scatter.5.cloned.1.call-update) | async-done | bytes 110608 | tf_op jit(solution)/shard_map/reduce_scatter | solution.py:246
  514.2 110.6 %reduce-scatter.9.cloned.1.call-done = bf16[96,768]{1,0:T(8,128)(2,1)} async-done(((bf16[3072,768]{1,0:T(8,128)(2,1)}), bf16[96,768]{1,0:T(8,128)(2,1)}) %reduce-scatter.9.cloned.1.call-update) | async-done | bytes 147472 | tf_op jit(solution)/shard_map/reduce_scatter | solution.py:165
  626.4 110.6 %reduce-scatter.11.cloned.1.call-done = bf16[24,3072]{1,0:T(8,128)(2,1)} async-done(((bf16[768,3072]{1,0:T(8,128)(2,1)}), bf16[24,3072]{1,0:T(8,128)(2,1)}) %reduce-scatter.11.cloned.1.call-update) | async-done | bytes 147472 | tf_op jit(solution)/shard_map/reduce_scatter | solution.py:165
  (107 shorter events, 41.0 us)
Async XLA Ops:
  7.2 66.4 %all-gather.5.cloned.1.call-start = ((), (), s32[]{:S(2)}) async-start(), calls=%async_computation.4 | async-start | bytes 3649536 | tf_op jit(solution)/shard_map/all_gather | solution.py:192
  7.9 121.5 %all-gather.7.cloned.1.call-start = ((), (), s32[]{:S(2)}) async-start(), calls=%async_computation.5 | async-start | bytes 1216512 | tf_op jit(solution)/shard_map/all_gather | solution.py:161
  8.7 186.2 %all-gather.9.cloned.1.call-start = ((), (), s32[]{:S(2)}) async-start(), calls=%async_computation.6 | async-start | bytes 4866048 | tf_op jit(solution)/shard_map/all_gather | solution.py:161
  9.4 250.1 %all-gather.11.cloned.1.call-start = ((), (), s32[]{:S(2)}) async-start(), calls=%async_computation.7 | async-start | bytes 4866048 | tf_op jit(solution)/shard_map/all_gather | solution.py:161
  10.0 441.4 %reduce-scatter.7.cloned.1.call-start = ((), (), s32[]{:S(2)}) async-start(), calls=%async_computation.9 | async-start | bytes 1216512 | tf_op jit(solution)/shard_map/reduce_scatter | solution.py:165
  13.7 245.8 %copy-start.8 = (f32[768]{0:T(1024)}, f32[768]{0:T(1024)S(1)}, u32[]{:S(2)}) copy-start(f32[768]{0:T(1024)S(1)} %get-tuple-element.53) | copy-start | bytes 9220
  91.2 38.2 %copy-start.21 = (f32[768]{0:T(1024)S(1)}, f32[768]{0:T(1024)}, u32[]{:S(2)}) copy-start(f32[768]{0:T(1024)} %param.18) | copy-start | bytes 9220
  133.2 170.1 %copy-start.1 = (f32[1024,768]{1,0:T(8,128)}, f32[1024,768]{1,0:T(8,128)S(1)}, u32[]{:S(2)}) copy-start(f32[1024,768]{1,0:T(8,128)S(1)} %get-tuple-element.45) | copy-start | bytes 9437188
  133.2 61.6 %copy-start.15 = (f32[768]{0:T(1024)S(1)}, f32[768]{0:T(1024)}, u32[]{:S(2)}) copy-start(f32[768]{0:T(1024)} %get-tuple-element.29) | copy-start | bytes 9220
  133.3 61.6 %copy-start.20 = (f32[3072]{0:T(1024)S(1)}, f32[3072]{0:T(1024)}, u32[]{:S(2)}) copy-start(f32[3072]{0:T(1024)} %param.20) | copy-start | bytes 36868
  133.8 169.5 %copy-start.11 = (f32[1024]{0:T(1024)}, f32[1024]{0:T(1024)S(1)}, u32[]{:S(2)}) copy-start(f32[1024]{0:T(1024)S(1)} %add_rsqrt_fusion.1) | copy-start | bytes 12292
  194.8 64.7 %copy-start.22 = (f32[768]{0:T(1024)S(1)}, f32[768]{0:T(1024)}, u32[]{:S(2)}) copy-start(f32[768]{0:T(1024)} %param.22) | copy-start | bytes 9220
  269.2 2.6 copy-start.7
  271.8 2.9 copy-start.17
  271.8 22.7 %slice-start = ((s8[4718592]{0:T(1024)(128)(4,1)}), s8[4194304]{0:T(1024)(128)(4,1)S(1)}, s32[]{:S(2)}) async-start(s8[4718592]{0:T(1024)(128)(4,1)} %bitcast.76), calls=%async_computation.12 | async-start | bytes 8388608
  274.1 20.4 %copy-start.4 = (f32[1024,768]{1,0:T(8,128)}, f32[1024,768]{1,0:T(8,128)S(1)}, u32[]{:S(2)}) copy-start(f32[1024,768]{1,0:T(8,128)S(1)} %get-tuple-element.31) | copy-start | bytes 9437188
  274.7 19.8 %copy-start.9 = (f32[768]{0:T(1024)S(1)}, f32[768]{0:T(1024)}, u32[]{:S(2)}) copy-start(f32[768]{0:T(1024)} %copy-done.8) | copy-start | bytes 9220
  274.7 19.8 %slice-start.1 = ((s8[4718592]{0:T(1024)(128)(4,1)}), s8[524288]{0:T(1024)(128)(4,1)S(1)}, s32[]{:S(2)}) async-start(s8[4718592]{0:T(1024)(128)(4,1)} %bitcast.76), calls=%async_computation.13 | async-start | bytes 1048576
  303.3 3.4 copy-start.23
  306.7 2.6 copy-start.19
  309.2 203.3 %reduce-scatter.5.cloned.1.call-start = ((), (), s32[]{:S(2)}) async-start(), calls=%async_computation.8 | async-start | bytes 3649536 | tf_op jit(solution)/shard_map/reduce_scatter | solution.py:246
  313.8 24.9 %copy-start.18 = (bf16[2,512,768]{2,1,0:T(8,128)(2,1)S(1)}, bf16[2,512,768]{2,1,0:T(8,128)(2,1)}, u32[]{:S(2)}) copy-start(bf16[2,512,768]{2,1,0:T(8,128)(2,1)} %param.13) | copy-start | bytes 4718596
  358.3 1.9 copy-start.2
  358.3 1.9 copy-start.12
  358.3 1.9 copy-start.16
  358.4 266.4 %reduce-scatter.9.cloned.1.call-start = ((), (), s32[]{:S(2)}) async-start(), calls=%async_computation.10 | async-start | bytes 4866048 | tf_op jit(solution)/shard_map/reduce_scatter | solution.py:165
  370.9 1.9 copy-start.5
  371.0 366.1 %reduce-scatter.11.cloned.1.call-start = ((), (), s32[]{:S(2)}) async-start(), calls=%async_computation.11 | async-start | bytes 4866048 | tf_op jit(solution)/shard_map/reduce_scatter | solution.py:165
  382.5 5.2 copy-start.13
  382.5 13.0 %copy-start.10 = (f32[768]{0:T(1024)S(1)}, f32[768]{0:T(1024)}, u32[]{:S(2)}) copy-start(f32[768]{0:T(1024)} %get-tuple-element.24) | copy-start | bytes 9220
  382.5 60.7 %copy-start.3 = (bf16[3,768,768]{2,1,0:T(8,128)(2,1)S(1)}, bf16[3,768,768]{2,1,0:T(8,128)(2,1)}, u32[]{:S(2)}) copy-start(bf16[3,768,768]{2,1,0:T(8,128)(2,1)} %reshape.144) | copy-start | bytes 10616836
  382.6 6.5 copy-start.14
  (2 other events, 3.1 us)
Sparse Core Ops, SparseCore 0:
  10.9 62.6 all-gather.4
  76.5 52.8 all-gather.6
  132.4 62.4 all-gather.8
  197.6 61.8 all-gather.10
  309.4 95.4 reduce-scatter.6
  410.1 102.4 reduce-scatter.4
  518.0 106.7 reduce-scatter.8
  630.3 106.7 reduce-scatter.10

commit v2 on v1

--- a/solution.py
+++ b/solution.py
@@ -14,6 +14,7 @@
 AXES = ("dp", "head")
 F32 = jnp.float32
 BF16 = jnp.bfloat16
+MESH = pl.DeviceIdType.MESH
 
 
 def dot(left, right, left_dim, right_dim):
@@ -157,12 +158,50 @@
     return inverse * (weighted - jnp.mean(weighted, axis=-1, keepdims=True) - normal * along)
 
 
-def gather(shard):
-    return lax.all_gather(shard, AXES, axis=0, tiled=True)
-
-
-def reduce_rows(term):
-    return lax.psum_scatter(term.astype(BF16), AXES, scatter_dimension=0, tiled=True)
+def sum_kernel(sizes, x_ref, out_ref, held, arrived, send_sem, recv_sem):
+    partners = []
+    for axis, size in sizes:
+        index = lax.axis_index(axis)
+        bit = 1
+        while bit < size:
+            partners.append({axis: index + bit - 2 * bit * ((index // bit) % 2)})
+            bit *= 2
+    barrier = pltpu.get_barrier_semaphore()
+    for partner in partners:
+        pl.semaphore_signal(barrier, 1, device_id=partner, device_id_type=MESH)
+    pl.semaphore_wait(barrier, len(partners))
+    held[0] = x_ref[...]
+    for step, partner in enumerate(partners):
+        copy = pltpu.make_async_remote_copy(
+            src_ref=held.at[step],
+            dst_ref=arrived.at[step],
+            send_sem=send_sem.at[step],
+            recv_sem=recv_sem.at[step],
+            device_id=partner,
+            device_id_type=MESH,
+        )
+        copy.start()
+        copy.wait()
+        held[step + 1] = held[step] + arrived[step]
+    out_ref[...] = held[len(partners)]
+
+
+def sum_everywhere(x, sizes):
+    steps = sum(size.bit_length() - 1 for _, size in sizes)
+    return pl.pallas_call(
+        functools.partial(sum_kernel, sizes),
+        out_shape=jax.ShapeDtypeStruct(x.shape, x.dtype),
+        in_specs=[pl.BlockSpec(memory_space=pltpu.VMEM)],
+        out_specs=pl.BlockSpec(memory_space=pltpu.VMEM),
+        scratch_shapes=[
+            pltpu.VMEM((steps + 1,) + x.shape, x.dtype),
+            pltpu.VMEM((steps,) + x.shape, x.dtype),
+            pltpu.SemaphoreType.DMA((steps,)),
+            pltpu.SemaphoreType.DMA((steps,)),
+        ],
+        compiler_params=pltpu.CompilerParams(collective_id=0, has_side_effects=True),
+        name="sum_everywhere",
+    )(x)
 
 
 def on_device(
@@ -189,15 +228,36 @@
     part, own_width = w_qkv.shape[1], w_qkv.shape[2]
     shard = (3, part, own_width)
 
-    gathered = lax.all_gather(w_qkv.reshape(3 * part, own_width), AXES, axis=0, tiled=True)
+    devices = dp_size * head_size
+    hidden_width = in_bias.shape[0]
+    out_part, in_part = width // devices, hidden_width // devices
+    chunks = hidden_width // width
+    back_part = chunks * out_part
+    qkv_part = 3 * part * own_width // width
+    packed = jnp.concatenate(
+        [
+            w_in.T,
+            w_back.reshape(chunks, width, out_part).transpose(0, 2, 1).reshape(back_part, width),
+            w_qkv.reshape(qkv_part, width),
+            w_out.T,
+        ]
+    )
+    gathered = lax.all_gather(packed, AXES, axis=0, tiled=False)
+    marks = (0, in_part, in_part + back_part, in_part + back_part + qkv_part)
+    in_full = gathered[:, : marks[1]].reshape(hidden_width, width)
+    back_full = (
+        gathered[:, marks[1] : marks[2]]
+        .reshape(devices, chunks, out_part, width)
+        .transpose(0, 2, 1, 3)
+        .reshape(width, hidden_width)
+    )
     qkv_full = (
-        gathered.reshape((dp_size, head_size) + shard)
+        gathered[:, marks[2] : marks[3]]
+        .reshape((dp_size, head_size) + shard)
         .transpose(2, 0, 3, 1, 4)
         .reshape(3, dp_size * part, head_size * own_width)
     )
-    out_full = gather(w_out.T)
-    in_full = gather(w_in.T)
-    back_full = gather(w_back.T)
+    out_full = gathered[:, marks[3] :].reshape(width, width)
 
     x = tokens.reshape(micro * local, width)
     segments = lax.dynamic_slice_in_dim(
@@ -225,15 +285,15 @@
     gain_two = jnp.sum(error * normal_two, axis=0)
     shift_two = jnp.sum(error, axis=0)
     grad_branch = grad_two.astype(BF16)
-    back_grad = reduce_rows(dot(grad_branch, activation, 0, 0))
+    back_term = dot(grad_branch, activation, 0, 0).astype(BF16)
     grad_pre = (slope * dot(grad_branch, back_full, 1, 0)).astype(BF16)
-    in_grad = reduce_rows(dot(grad_pre, hidden_low, 0, 0))
+    in_term = dot(grad_pre, hidden_low, 0, 0).astype(BF16)
     grad_hidden = grad_two + dot(grad_pre, in_full, 1, 0)
     grad_one = norm_back(normal_one, inverse_one, grad_hidden, norm_gains[0])
     gain_one = jnp.sum(grad_hidden * normal_one, axis=0)
     shift_one = jnp.sum(grad_hidden, axis=0)
     grad_attn = grad_one.astype(BF16)
-    out_grad = reduce_rows(dot(grad_attn, context, 0, 0))
+    out_term = dot(grad_attn, context, 0, 0).astype(BF16)
     grad_context = dot(grad_attn, out_full, 1, 0).astype(BF16)
     grad_qkv = attend_back(segments, qkv, totals, grad_context)
     term = jnp.einsum("td,ctf->cdf", x, grad_qkv, preferred_element_type=F32)
@@ -241,9 +301,23 @@
         term.astype(BF16)
         .reshape(3, dp_size, part, head_size, own_width)
         .transpose(1, 3, 0, 2, 4)
-        .reshape(dp_size * head_size * 3 * part, own_width)
-    )
-    qkv_grad = lax.psum_scatter(term, AXES, scatter_dimension=0, tiled=True)
+        .reshape(devices, qkv_part, width)
+    )
+    back_term = (
+        back_term.reshape(devices, out_part, chunks, width)
+        .transpose(0, 2, 1, 3)
+        .reshape(devices, back_part, width)
+    )
+    terms = jnp.concatenate(
+        [
+            in_term.reshape(devices, in_part, width),
+            back_term,
+            term,
+            out_term.reshape(devices, out_part, width),
+        ],
+        axis=1,
+    )
+    summed = lax.psum_scatter(terms, AXES, scatter_dimension=0, tiled=False).astype(F32)
     x_grad = grad_one + jnp.einsum(
         "ctf,cdf->td", grad_qkv, qkv_full, preferred_element_type=F32
     )
@@ -260,8 +334,9 @@
             shift_two,
         ]
     )
-    small = lax.psum(small, AXES)
-    hidden_width = in_bias.shape[0]
+    small = sum_everywhere(
+        small.reshape(-1, 128), (("dp", dp_size), ("head", head_size))
+    ).reshape(-1)
     cuts, at = [], 0
     for size in (2 * width, width, hidden_width, width, 2 * width, 2 * width):
         cuts.append(small[at : at + size])
@@ -269,13 +344,16 @@
     return (
         out.reshape(tokens.shape),
         x_grad.reshape(tokens.shape),
-        qkv_grad.astype(F32).reshape(shard),
+        summed[marks[2] : marks[3]].reshape(shard),
         cuts[0].reshape(2, width),
-        out_grad.astype(F32).T,
+        summed[marks[3] :].T,
         cuts[1],
-        in_grad.astype(F32).T,
+        summed[: marks[1]].T,
         cuts[2],
-        back_grad.astype(F32).T,
+        summed[marks[1] : marks[2]]
+        .reshape(chunks, out_part, width)
+        .transpose(0, 2, 1)
+        .reshape(hidden_width, out_part),
         cuts[3],
         cuts[4].reshape(2, width),
         cuts[5].reshape(2, width),

time: 751 us -> 510 us (0.68)
  waiting for transfers between devices: 466 us -> 216 us
  blocking collectives: 39.8 us -> 0 us
  local copies, waits for them, and re-layouts: 51.1 us -> 88.8 us
  Pallas kernels: 43.5 us -> 59.9 us
  matrix products: 111 us -> 97.3 us
    reduce_scatter x4 -> x1, waiting for transfers between devices: 281 us -> 116 us  [on_device(): lax.psum_scatter(terms, AXES, scatter_dimension=0, tiled=False).astype(F32)]
    all_gather x4 -> x1, waiting for transfers between devices: 182 us -> 99.9 us  [on_device(): gathered = lax.all_gather(packed, AXES, axis=0, tiled=False)]
    psum x1 -> x0, blocking collectives: 39.8 us -> none  [on_device(): small = lax.psum(small, AXES)]
    reshape x1 -> x10, local copies, waits for them, and re-layouts: 4.18 us -> 22.4 us  [the longest x1 9.74 us: on_device(): back_term.reshape(devices, out_part, chunks, width).transpose(0, 2, 1, 3)]
    pallas_call x0 -> x1, Pallas kernels: none -> 16.1 us  [sum_everywhere(): pl.pallas_call(functools.partial(sum_kernel, sizes), out_shape=jax.ShapeD...]
    dot_general x9, matrix products: 86.9 us -> 72.5 us  [dot(): lax.dot_general(left, right, (((left_dim,), (right_dim,)), ((), ())), pre...]
    slice x0 -> x5, local copies, waits for them, and re-layouts: none -> 13.6 us  [the longest x1 8.04 us: on_device(): gathered[:, marks[1]:marks[2]].reshape(devices, chunks, out_part, width)]
    concatenate x0 -> x2, other arithmetic: none -> 12.6 us  [the longest x1 10.8 us: on_device(): jnp.concatenate([in_term.reshape(devices, in_part, width), back_term, ter...]
  transfers between devices with their start and end apart: 8 -> 2, of which waited for: 7 -> 2; matrix products, arithmetic and copies ran while one was open for 17% -> 7% of each run, Pallas kernels for 6% -> 3%
where the time goes in v2:
time: 510 us; the launch traced here: 501 us
  waiting for transfers between devices  216 us (42%)
  matrix products  97.3 us (19%)
  local copies, waits for them, and re-layouts  88.8 us (17%)
  Pallas kernels  59.9 us (12%)
  other arithmetic  24.6 us (5%)
  between operations  14.9 us (3%)
    reduce_scatter x1, waiting for transfers between devices, on_device(): lax.psum_scatter(terms, AXES, scatter_dimension=0, tiled=False).astype(F32)  116 us
    all_gather x1, waiting for transfers between devices, on_device(): gathered = lax.all_gather(packed, AXES, axis=0, tiled=False)  99.9 us
    dot_general x9, matrix products, dot(): lax.dot_general(left, right, (((left_dim,), (right_dim,)), ((), ())), pre...  72.5 us
    pallas_call x1, Pallas kernels, attend_back(): pl.pallas_call(attend_back_kernel, grid=(rows, pairs), in_specs=[s['row']...  24.6 us
    pallas_call x1, Pallas kernels, attend(): pl.pallas_call(attend_kernel, grid=(rows, pairs), in_specs=[s['row'], s['...  19.2 us
    pallas_call x1, Pallas kernels, sum_everywhere(): pl.pallas_call(functools.partial(sum_kernel, sizes), out_shape=jax.ShapeD...  16.1 us
    unnamed x67, local copies, waits for them, and re-layouts  13.2 us
    concatenate x1, other arithmetic, on_device(): jnp.concatenate([in_term.reshape(devices, in_part, width), back_term, ter...  10.8 us
  transfers between devices with their start and end apart: 2, of which 2 were waited for; matrix products, arithmetic and copies ran while one was open for 7% of the time, Pallas kernels for 3%

profile of v2, /device:TPU:0, one launch (start us, length us, event | category | flops | bytes accessed | tf_op | source)
XLA Modules:
  0.0 501.3 jit_solution(4335102764651635879)
XLA Ops:
  16.9 99.9 %all-gather.3.cloned.1.call-done = bf16[9216,768]{1,0:T(8,128)(2,1)} async-done(((bf16[288,768]{1,0:T(8,128)(2,1)}), bf16[9216,768]{1,0:T(8,128)(2,1)}) %all-gather.3.cloned.1.call-update) | async-done | bytes 14155792 | tf_op jit(solution)/shard_map/all_gather | solution.py:245
  119.0 2.4 slice.116
  121.4 8.0 %fusion.25 = (bf16[32,96,768]{2,1,0:T(8,128)(2,1)}, bf16[32,96,768]{2,1,0:T(8,128)(2,1)}) fusion(bf16[32,288,768]{2,1,0:T(8,128)(2,1)} %bitcast.103), kind=kLoop, calls=%fused_computation.84 | loop fusion | bytes 18874368 | tf_op jit(solution)/shard_map/slice | solution.py:249
  129.4 3.3 reshape.180
  132.7 4.9 copy.43
  137.6 4.0 reshape.181
  141.6 8.5 %fusion.7.qkv_ref = bf16[3,1024,768]{2,1,0:T(8,128)(2,1)} fusion(f32[3,768]{1,0:T(4,128)} %pad_maximum_fusion.2, bf16[1024,768,1]{1,0,2:T(8,128)(2,1)} %bitcast.123, bf16[3,768,768]{2,1,0:T(8,128)(2,1)} %reshape.181), kind=kOutput, calls=%fused_computation.15 | convolution fusion | flops 3628597248 | bytes 9839616 | tf_op jit(solution)/shard_map/td,cdf->ctf/dot_general | solution.py:268
  150.1 19.2 %attend.1 = (bf16[1024,768]{1,0:T(8,128)(2,1)}, f32[2,6,8,512]{3,2,1,0:T(8,128)}) custom-call(s32[2,1,512]{2,1,0:T(1,128)} %get-tuple-element.35.seg_row, s32[2,512,1]{2,1,0:T(8,128)} %broadcast_in_dim_reshape.5.seg_col, bf16[3,1024,768]{2,1,0:T(8,128)(2,1)} %fusion.7.qkv_ref), custom_call_target="tpu_custom_call" | custom-call | flops 3221225472 | bytes 7077888 | tf_op jit(solution)/shard_map/attend/pallas_call | solution.py:99
  169.3 3.6 fusion.28
  173.5 2.3 copy.47
  177.0 15.4 %multiply_convert_fusion = (bf16[1024,3072]{1,0:T(8,128)(2,1)S(1)}, f32[1024,3072]{1,0:T(8,128)}) fusion(f32[3072]{0:T(1024)S(1)} %copy-done.16, bf16[3072,768]{1,0:T(8,128)(2,1)S(1)} %bitcast.109, f32[1024,768]{1,0:T(8,128)S(1)} %get-tuple-element.47, f32[768]{0:T(1024)S(1)} %copy-done.12, f32[768]{0:T(1024)S(1)} %get-tuple-element.55, ...), kind=kOutput, calls=%fused_computation.11 | convolution fusion | flops 4904976384 | bytes 26765312 | tf_op jit(solution)/shard_map/dot_general | solution.py:21
  192.5 5.5 %fusion.29 = (f32[1024]{0:T(1024)S(1)}, f32[1024,768]{1,0:T(8,128)S(1)}) fusion(f32[768]{0:T(1024)S(1)} %copy-done.18, bf16[1024,3072]{1,0:T(8,128)(2,1)S(1)} %get-tuple-element.48, bf16[768,3072]{1,0:T(8,128)(2,1)S(1)} %bitcast.105, f32[768]{0:T(1024)S(1)} %copy-done.12, f32[768]{0:T(1024)S(1)} %get-tuple-element.55, f32[1024]{0:T(1024)S(1)} %add_rsqrt_fusion.1, ...), kind=kOutput, calls=%fused_computation.88 | convolution fusion | flops 4837342208 | bytes 17323008 | tf_op jit(solution)/shard_map/dot_general | solution.py:21
  201.2 2.3 convert_reduce_fusion.2
  203.5 7.0 %convolution_convert_fusion = bf16[768,3072]{1,0:T(8,128)(2,1)} fusion(bf16[1024,3072]{1,0:T(8,128)(2,1)S(1)} %bitcast.128, f32[1024,768]{1,0:T(8,128)S(1)} %get-tuple-element.31), kind=kOutput, calls=%fused_computation.13 | convolution fusion | flops 4834983936 | bytes 14155776 | tf_op jit(solution)/shard_map/dot_general | solution.py:21
  210.5 18.5 %convert_reduce_fusion = (f32[3072]{0:T(1024)}, bf16[1024,3072]{1,0:T(8,128)(2,1)}) fusion(bf16[768,3072]{1,0:T(8,128)(2,1)S(1)} %bitcast.106, f32[1024,768]{1,0:T(8,128)S(1)} %get-tuple-element.31, f32[1024,3072]{1,0:T(8,128)} %get-tuple-element.49, f32[3072]{0:T(1024)S(1)} %copy-done.16), kind=kOutput, calls=%fused_computation.10 | convolution fusion | flops 4917556224 | bytes 26763264 | tf_op jit(solution)/shard_map/dot_general | solution.py:21
  229.0 10.9 %convolution_convert_fusion.1 = bf16[3072,768]{1,0:T(8,128)(2,1)} fusion(bf16[1024,3072]{1,0:T(8,128)(2,1)} %get-tuple-element.54, f32[1024,768]{1,0:T(8,128)S(1)} %get-tuple-element.47, f32[768]{0:T(1024)S(1)} %copy-done.12, f32[768]{0:T(1024)S(1)} %copy-done.7, f32[1024]{0:T(1024)S(1)} %add_rsqrt_fusion.1, f32[1024]{0:T(1024)S(1)} %broadcast_multiply_fusion.4), kind=kOutput, calls=%fused_computation.14 | convolution fusion | flops 4838129664 | bytes 14170112 | tf_op jit(solution)/shard_map/dot_general | solution.py:21
  239.8 6.5 %multiply_reduce_fusion = (f32[768]{0:T(1024)}, f32[1024]{0:T(1024)S(1)}, f32[1024]{0:T(1024)S(1)}, f32[768]{0:T(1024)}, f32[1024,768]{1,0:T(8,128)S(1)}) fusion(f32[1024,768]{1,0:T(8,128)S(1)} %get-tuple-element.47, f32[1024]{0:T(1024)S(1)} %add_rsqrt_fusion.1, f32[1024]{0:T(1024)S(1)} %broadcast_multiply_fusion.4, f32[768]{0:T(1024)S(1)} %copy-done.7, ...), kind=kOutput, calls=%fused_computation.29 | convolution fusion | flops 4839698432 | bytes 20472832 | tf_op jit(solution)/shard_map/dot_general | solution.py:21
  247.7 2.6 convolution_convert_fusion.2.grad_ref
  250.3 2.5 convolution_convert_fusion.3
  252.8 9.7 %reshape.189 = bf16[32,24,4,768]{3,2,1,0:T(4,128)(2,1)} reshape(bf16[768,3072]{1,0:T(8,128)(2,1)} %convolution_convert_fusion) | data formatting | bytes 9437184 | tf_op jit(solution)/shard_map/reshape | solution.py:307
  262.6 5.4 %copy.49 = bf16[32,4,24,768]{3,2,1,0:T(8,128)(2,1)} copy(bf16[32,4,24,768]{3,1,2,0:T(4,128)(2,1)} %bitcast.95) | data formatting | bytes 9437184 | tf_op jit(solution)/shard_map/transpose | solution.py:308
  268.0 24.6 %attend_back.1 = bf16[3,1024,768]{2,1,0:T(8,128)(2,1)} custom-call(s32[2,1,512]{2,1,0:T(1,128)} %get-tuple-element.35.seg_row, s32[2,512,1]{2,1,0:T(8,128)} %broadcast_in_dim_reshape.5.seg_col, bf16[3,1024,768]{2,1,0:T(8,128)(2,1)} %fusion.7.qkv_ref, f32[2,6,8,512]{3,2,1,0:T(8,128)} %get-tuple-element.15.total_ref, ...), custom_call_target="tpu_custom_call" | custom-call | flops 8053063680 | bytes 11796480 | tf_op jit(solution)/shard_map/attend_back/pallas_call | solution.py:121
  292.6 7.9 %convert_bitcast_fusion = bf16[3,768,768]{1,2,0:T(8,128)(2,1)} fusion(bf16[3,1024,768]{2,1,0:T(8,128)(2,1)} %attend_back.1, bf16[1024,768,1]{1,0,2:T(8,128)(2,1)S(1)} %bitcast.125), kind=kOutput, calls=%fused_computation.16 | convolution fusion | flops 3625648128 | bytes 9830400 | tf_op jit(solution)/shard_map/td,ctf->cdf/dot_general | solution.py:299
  300.4 4.3 copy.51
  304.7 3.1 reshape.191
  307.8 4.2 copy.52
  312.0 4.8 reshape.192
  316.9 10.8 %pad_maximum_fusion = bf16[32,288,768]{2,1,0:T(8,128)(2,1)} fusion(bf16[32,24,768]{2,1,0:T(8,128)(2,1)} %bitcast.112, bf16[32,72,768]{2,1,0:T(8,128)(2,1)S(1)} %reshape.192, bf16[32,96,768]{2,1,0:T(8,128)(2,1)} %bitcast.93, bf16[32,96,768]{2,1,0:T(8,128)(2,1)} %bitcast.104), kind=kLoop, calls=%fused_computation.2 | loop fusion | flops 56623104 | bytes 28311552 | tf_op jit(solution)/shard_map/concatenate | solution.py:311
  327.8 2.5 convert_reduce_fusion.4
  342.1 16.1 %sum_everywhere.1 = f32[72,128]{1,0:T(8,128)} custom-call(f32[72,128]{1,0:T(8,128)} %bitcast.24.x_ref), custom_call_target="tpu_custom_call" | custom-call | tf_op jit(solution)/shard_map/sum_everywhere/pallas_call | solution.py:191
  364.7 8.5 %bitcast_add_fusion = f32[1024,768]{1,0:T(8,128)} fusion(f32[1024,768]{1,0:T(8,128)} %copy-done.3, bf16[3,1024,768]{2,1,0:T(8,128)(2,1)} %attend_back.1, bf16[3,768,768]{2,1,0:T(8,128)(2,1)S(1)} %copy-done.2), kind=kOutput, calls=%fused_computation.17 | convolution fusion | flops 3624665088 | bytes 14548992 | tf_op jit(solution)/shard_map/ctf,cdf->td/dot_general | solution.py:321
  373.2 115.7 %reduce-scatter.2.cloned.1.call-done = bf16[1,288,768]{2,1,0:T(8,128)(2,1)} async-done(((bf16[32,288,768]{2,1,0:T(8,128)(2,1)}), bf16[1,288,768]{2,1,0:T(8,128)(2,1)}) %reduce-scatter.2.cloned.1.call-update) | async-done | bytes 442384 | tf_op jit(solution)/shard_map/reduce_scatter | solution.py:320
  (113 shorter events, 41.4 us)
Async XLA Ops:
  7.2 7.7 %copy-start = (bf16[2,512,768]{2,1,0:T(8,128)(2,1)S(1)}, bf16[2,512,768]{2,1,0:T(8,128)(2,1)}, u32[]{:S(2)}) copy-start(bf16[2,512,768]{2,1,0:T(8,128)(2,1)} %param.25) | copy-start | bytes 4718596
  7.2 9.0 %copy-start.11 = (f32[2,768]{1,0:T(2,128)S(1)}, f32[2,768]{1,0:T(2,128)}, u32[]{:S(2)}) copy-start(f32[2,768]{1,0:T(2,128)} %param.16) | copy-start | bytes 18436
  7.2 109.6 %all-gather.3.cloned.1.call-start = ((), (), s32[]{:S(2)}) async-start(), calls=%async_computation.2 | async-start | bytes 14598144 | tf_op jit(solution)/shard_map/all_gather | solution.py:245
  11.1 477.8 %reduce-scatter.2.cloned.1.call-start = ((), (), s32[]{:S(2)}) async-start(), calls=%async_computation.1 | async-start | bytes 14598144 | tf_op jit(solution)/shard_map/reduce_scatter | solution.py:320
  14.8 177.6 %copy-start.6 = (f32[768]{0:T(1024)}, f32[768]{0:T(1024)S(1)}, u32[]{:S(2)}) copy-start(f32[768]{0:T(1024)S(1)} %get-tuple-element.55) | copy-start | bytes 9220
  150.1 19.2 %copy-start.5 = (bf16[32,24,768]{2,1,0:T(8,128)(2,1)S(1)}, bf16[32,24,768]{2,1,0:T(8,128)(2,1)}, u32[]{:S(2)}) copy-start(bf16[32,24,768]{2,1,0:T(8,128)(2,1)} %slice.116) | copy-start | bytes 3538948
  150.1 19.3 %copy-start.17 = (f32[768]{0:T(1024)S(1)}, f32[768]{0:T(1024)}, u32[]{:S(2)}) copy-start(f32[768]{0:T(1024)} %param.18) | copy-start | bytes 9220
  169.3 4.2 slice-start
  169.3 4.2 slice-start.1
  173.5 3.4 slice-start.2
  175.9 1.1 slice-start.3
  175.9 1.1 copy-start.12
  175.9 1.1 copy-start.16
  177.0 15.5 %copy-start.18 = (f32[768]{0:T(1024)S(1)}, f32[768]{0:T(1024)}, u32[]{:S(2)}) copy-start(f32[768]{0:T(1024)} %param.22) | copy-start | bytes 9220
  192.4 5.5 %copy-start.19 = (bf16[1024,3072]{1,0:T(8,128)(2,1)}, bf16[1024,3072]{1,0:T(8,128)(2,1)S(1)}, u32[]{:S(2)}) copy-start(bf16[1024,3072]{1,0:T(8,128)(2,1)S(1)} %get-tuple-element.48) | copy-start | bytes 18874372
  198.0 1.4 copy-start.1
  199.4 4.1 slice-start.4
  201.2 2.3 slice-start.5
  210.5 18.5 %copy-start.7 = (f32[768]{0:T(1024)S(1)}, f32[768]{0:T(1024)}, u32[]{:S(2)}) copy-start(f32[768]{0:T(1024)} %copy-done.6) | copy-start | bytes 9220
  229.0 10.9 %copy-start.21 = (bf16[1024,3072]{1,0:T(8,128)(2,1)S(1)}, bf16[1024,3072]{1,0:T(8,128)(2,1)}, u32[]{:S(2)}) copy-start(bf16[1024,3072]{1,0:T(8,128)(2,1)} %get-tuple-element.54) | copy-start | bytes 18874372
  247.7 2.6 copy-start.3
  247.7 2.6 copy-start.20
  268.0 24.6 %copy-start.15 = (bf16[2,512,768]{2,1,0:T(8,128)(2,1)S(1)}, bf16[2,512,768]{2,1,0:T(8,128)(2,1)}, u32[]{:S(2)}) copy-start(bf16[2,512,768]{2,1,0:T(8,128)(2,1)} %param.13) | copy-start | bytes 4718596
  327.7 37.0 %copy-start.2 = (bf16[3,768,768]{2,1,0:T(8,128)(2,1)S(1)}, bf16[3,768,768]{2,1,0:T(8,128)(2,1)}, u32[]{:S(2)}) copy-start(bf16[3,768,768]{2,1,0:T(8,128)(2,1)} %reshape.181) | copy-start | bytes 10616836
  327.7 10.4 %copy-start.9 = (f32[768]{0:T(1024)S(1)}, f32[768]{0:T(1024)}, u32[]{:S(2)}) copy-start(f32[768]{0:T(1024)} %get-tuple-element.18) | copy-start | bytes 9220
  327.7 13.0 %copy-start.8 = (f32[768]{0:T(1024)S(1)}, f32[768]{0:T(1024)}, u32[]{:S(2)}) copy-start(f32[768]{0:T(1024)} %get-tuple-element.24) | copy-start | bytes 9220
  327.8 6.5 %copy-start.10 = (f32[3072]{0:T(1024)S(1)}, f32[3072]{0:T(1024)}, u32[]{:S(2)}) copy-start(f32[3072]{0:T(1024)} %get-tuple-element.53) | copy-start | bytes 36868
  327.8 9.1 %copy-start.14 = (f32[768]{0:T(1024)S(1)}, f32[768]{0:T(1024)}, u32[]{:S(2)}) copy-start(f32[768]{0:T(1024)} %get-tuple-element.16) | copy-start | bytes 9220
  327.8 11.7 %copy-start.13 = (f32[768]{0:T(1024)S(1)}, f32[768]{0:T(1024)}, u32[]{:S(2)}) copy-start(f32[768]{0:T(1024)} %get-tuple-element.23) | copy-start | bytes 9220
  488.9 4.3 copy-start.4
Sparse Core Ops, SparseCore 0:
  11.5 105.2 all-gather.2
  327.9 160.9 reduce-scatter.1
